TPU v7x, 128 devices: a whole 4x4x4 slice. The times are simulated.
128 devices in a mesh: pipe: 16 (over y_lo, z, core), seq: 8 (over x, y_hi).
Axes of the slice: x: 4, y: 4 (y_hi: 2, y_lo: 2; y = y_hi * 2 + y_lo), z: 4, core: 2. Of those that a mesh axis runs over, the one named last changes fastest.
Arguments:
- x_fwd: float32 [16, 1024, 2048], P('pipe', 'seq'), may hold values from -12 to 12
- x_bwd: float32 [16, 1024, 2048], P('pipe', 'seq'), may hold values from -12 to 12
- grad_in: float32 [16, 1024, 2048], P('pipe', 'seq'), may hold values from -6 to 6
- gain: float32 [16, 2048], P('pipe'), may hold values from 0.25 to 1.75
- w_query: bfloat16 [16, 2048, 2048], P('pipe', None, 'seq'), may hold values from -2 to 2
- w_key: bfloat16 [16, 2048, 2048], P('pipe', None, 'seq'), may hold values from -2 to 2
- w_value: bfloat16 [16, 2048, 2048], P('pipe', None, 'seq'), may hold values from -0.125 to 0.125
- w_out: bfloat16 [16, 2048, 2048], P('pipe', None, 'seq'), may hold values from -0.125 to 0.125
Outputs:
- act_next: float32 [16, 1024, 2048], P('pipe', 'seq')
- grad_prev: float32 [16, 1024, 2048], P('pipe', 'seq')
All inputs are finite; a program needn't handle non-finite values.
Results may differ from a plain program's by a relative error of at most 0.012.
The roundings to bfloat16 on the way count: a program that leaves them out, or rounds other values in their place, can miss the bound.
Values may be sent and summed in bfloat16 or wider, within the bound.
A program may use at most 192 MiB of HBM per device.

v0:
```python
import jax
import jax.numpy as jnp
from jax import lax
from jax.sharding import PartitionSpec as P

HD = 128


def passed_along(value, axis, steps):
    count = lax.axis_size(axis)
    pairs = [(source, (source + steps) % count) for source in range(count)]
    return lax.ppermute(value, axis, pairs)


def rope_tables(positions):
    half_dim = HD // 2
    inverse = 10000.0 ** (-(jnp.arange(half_dim).astype(jnp.float32) * 2.0 / HD))
    angles = positions.astype(jnp.float32)[:, None] * inverse[None, :]
    return (jnp.cos(angles)[:, None, :], jnp.sin(angles)[:, None, :])


def rotate(values, cosine, sine_table):
    shaped = values.reshape(values.shape[0], -1, HD)
    first_half = shaped[..., : HD // 2]
    second_half = shaped[..., HD // 2 :]
    output = jnp.concatenate(
        [
            first_half * cosine - second_half * sine_table,
            second_half * cosine + first_half * sine_table,
        ],
        -1,
    )
    return output.reshape(values.shape)


def rotate_back(values, cosine, sine_table):
    shaped = values.reshape(values.shape[0], -1, HD)
    first_half = shaped[..., : HD // 2]
    second_half = shaped[..., HD // 2 :]
    output = jnp.concatenate(
        [
            first_half * cosine + second_half * sine_table,
            second_half * cosine - first_half * sine_table,
        ],
        -1,
    )
    return output.reshape(values.shape)


def normalize(inputs, gain_row):
    inv_rms = lax.rsqrt(jnp.mean(inputs * inputs, -1, keepdims=True) + 1e-05)
    return ((inputs * inv_rms * gain_row).astype(jnp.bfloat16), inv_rms)


def times_t(left, right):
    return lax.dot_general(
        left, right, (((1,), (1,)), ((), ())), preferred_element_type=jnp.float32
    )


def split_heads(values):
    return values.reshape(values.shape[0], -1, HD)


def attend(query, key_rows, value_rows):
    length = query.shape[0]
    score_scale = HD ** (-0.5)
    key_heads = split_heads(key_rows)
    value_heads = split_heads(value_rows)
    query_blocks = split_heads(query).reshape(length // length, length, -1, HD)

    def one_block(query_block):
        scores = (
            jnp.einsum("qhd,khd->hqk", query_block, key_heads, preferred_element_type=jnp.float32)
            * score_scale
        )
        probs = jax.nn.softmax(scores, axis=-1)
        output = jnp.einsum(
            "hqk,khd->qhd",
            probs.astype(jnp.bfloat16),
            value_heads,
            preferred_element_type=jnp.float32,
        )
        return output.astype(jnp.bfloat16)

    return lax.map(one_block, query_blocks).reshape(length, -1)


def attend_back(query, key_rows, value_rows, grad_out, cosine, sine_table):
    length = query.shape[0]
    score_scale = HD ** (-0.5)
    key_heads = split_heads(key_rows)
    value_heads = split_heads(value_rows)
    query_blocks = split_heads(query).reshape(length // length, length, -1, HD)
    grad_blocks = split_heads(grad_out).reshape(length // length, length, -1, HD)

    def step(totals, operands):
        query_block, grad_block = operands
        scores = (
            jnp.einsum("qhd,khd->hqk", query_block, key_heads, preferred_element_type=jnp.float32)
            * score_scale
        )
        probs = jax.nn.softmax(scores, axis=-1)
        value_grad = jnp.einsum(
            "hqk,qhd->khd",
            probs.astype(jnp.bfloat16),
            grad_block,
            preferred_element_type=jnp.float32,
        )
        prob_grad = jnp.einsum(
            "qhd,khd->hqk", grad_block, value_heads, preferred_element_type=jnp.float32
        )
        row_delta = jnp.sum(probs * prob_grad, -1, keepdims=True)
        score_grad = (probs * (prob_grad - row_delta) * score_scale).astype(jnp.bfloat16)
        query_grad = jnp.einsum(
            "hqk,khd->qhd", score_grad, key_heads, preferred_element_type=jnp.float32
        )
        key_grad = jnp.einsum(
            "hqk,qhd->khd", score_grad, query_block, preferred_element_type=jnp.float32
        )
        return ((totals[0] + key_grad, totals[1] + value_grad), query_grad)

    zero_heads = jnp.zeros(key_heads.shape, jnp.float32)
    (key_total, value_total), query_grads = lax.scan(
        step, (zero_heads, zero_heads), (query_blocks, grad_blocks)
    )
    query_grad = rotate_back(query_grads.reshape(length, -1), cosine, sine_table).astype(
        jnp.bfloat16
    )
    key_grad = rotate_back(key_total.reshape(length, -1), cosine, sine_table).astype(jnp.bfloat16)
    return (query_grad, key_grad, value_total.reshape(length, -1).astype(jnp.bfloat16))


def to_tokens(values):
    return lax.all_to_all(values, "seq", split_axis=1, concat_axis=2, tiled=True)


def shards(x_fwd, x_bwd, grad_in, gain, w_query, w_key, w_value, w_out):
    act_in = x_fwd[0]
    saved_in = x_bwd[0]
    grad = grad_in[0]
    gain_row = gain[0]
    local_rows = act_in.shape[0]
    length = local_rows * lax.axis_size("seq")
    normed_fwd, inv_fwd = normalize(act_in, gain_row)
    normed_bwd, inv_bwd = normalize(saved_in, gain_row)
    grad_low = grad.astype(jnp.bfloat16)
    full_cos, full_sin = rope_tables(jnp.arange(length))
    all_query, all_key, all_value, all_out = (
        lax.all_gather(w_query[0], "seq", axis=1, tiled=True),
        lax.all_gather(w_key[0], "seq", axis=1, tiled=True),
        lax.all_gather(w_value[0], "seq", axis=1, tiled=True),
        lax.all_gather(w_out[0], "seq", axis=1, tiled=True),
    )
    local_cos, local_sin = rope_tables(lax.axis_index("seq") * local_rows + jnp.arange(local_rows))

    def project_local(normed):
        query = rotate(
            jnp.dot(normed, all_query, preferred_element_type=jnp.float32), local_cos, local_sin
        ).astype(jnp.bfloat16)
        key_rows = rotate(
            jnp.dot(normed, all_key, preferred_element_type=jnp.float32), local_cos, local_sin
        ).astype(jnp.bfloat16)
        value_rows = jnp.dot(normed, all_value, preferred_element_type=jnp.float32).astype(
            jnp.bfloat16
        )
        return [query, key_rows, value_rows]

    attn_grad = jnp.dot(grad_low, all_out, preferred_element_type=jnp.float32).astype(jnp.bfloat16)
    pieces = jnp.stack(project_local(normed_fwd) + project_local(normed_bwd) + [attn_grad])
    head_view = lax.all_to_all(pieces, "seq", split_axis=2, concat_axis=1, tiled=True)
    attn = attend(head_view[0], head_view[1], head_view[2])
    attn_tokens = to_tokens(attn[None])[0]
    branch = times_t(attn_tokens, all_out)
    query_grad, key_grad, value_grad = attend_back(
        head_view[3], head_view[4], head_view[5], head_view[6], full_cos, full_sin
    )
    grad_tokens = to_tokens(jnp.stack([query_grad, key_grad, value_grad]))
    d_normed = (
        times_t(grad_tokens[0], all_query)
        + times_t(grad_tokens[1], all_key)
        + times_t(grad_tokens[2], all_value)
    )
    act_out = act_in + branch
    gain_grad = d_normed * gain_row
    d_input = inv_bwd * gain_grad - saved_in * inv_bwd * inv_bwd * inv_bwd * jnp.mean(
        saved_in * gain_grad, -1, keepdims=True
    )
    sent_forward = passed_along(act_out.astype(jnp.bfloat16), "pipe", 1).astype(act_out.dtype)
    sent_backward = passed_along((grad + d_input).astype(jnp.bfloat16), "pipe", -1).astype(
        jnp.float32
    )
    return (sent_forward[None], sent_backward[None])


def solution(mesh):
    placed = (
        P("pipe", "seq", None),
        P("pipe", "seq", None),
        P("pipe", "seq", None),
        P("pipe", None),
        P("pipe", None, "seq"),
        P("pipe", None, "seq"),
        P("pipe", None, "seq"),
        P("pipe", None, "seq"),
    )
    return jax.shard_map(
        shards,
        mesh=mesh,
        in_specs=placed,
        out_specs=(P("pipe", "seq", None), P("pipe", "seq", None)),
        check_vma=False,
    )
```

profile of v0, /device:TPU:1, one launch (start us, length us, event | category | flops | bytes accessed | tf_op | source)
XLA Modules:
  0.0 765.0 jit_solution(12762140533666074192)
XLA Ops:
  13.0 118.5 %all-gather.11.cloned.1.call-done = bf16[1,2048,2048]{2,1,0:T(8,128)(2,1)} async-done(((bf16[1,2048,256]{2,1,0:T(8,128)(2,1)}), bf16[1,2048,2048]{2,1,0:T(8,128)(2,1)}) %all-gather.11.cloned.1.call-update) | async-done | bytes 8388624 | tf_op jit(solution)/shard_map/all_gather | solution.py:151
  131.5 12.4 %copy.67 = bf16[2048,2048]{1,0:T(8,128)(2,1)} copy(bf16[2048,2048]{0,1:T(8,128)(2,1)} %bitcast.212) | data formatting | bytes 16777216 | tf_op jit(solution)/shard_map/dot_general | solution.py:162
  143.8 108.1 %all-gather.9.cloned.1.call-done = bf16[1,2048,2048]{2,1,0:T(8,128)(2,1)} async-done(((bf16[1,2048,256]{2,1,0:T(8,128)(2,1)}), bf16[1,2048,2048]{2,1,0:T(8,128)(2,1)}) %all-gather.9.cloned.1.call-update) | async-done | bytes 8388624 | tf_op jit(solution)/shard_map/all_gather | solution.py:150
  251.9 12.4 %copy.66 = bf16[2048,2048]{1,0:T(8,128)(2,1)} copy(bf16[2048,2048]{0,1:T(8,128)(2,1)} %bitcast.213) | data formatting | bytes 16777216 | tf_op jit(solution)/shard_map/dot_general | solution.py:159
  264.3 6.5 fusion.112
  270.9 2.5 fusion.116
  273.6 2.5 fusion.114
  276.1 2.5 fusion.118
  278.5 1.5 subtract_convert_fusion.2
  282.4 2.2 pad_maximum_fusion.1
  284.5 2.0 copy.68
  286.6 2.0 copy.69
  288.6 1.9 constant_dynamic-update-slice_fusion.3
  290.5 1.9 constant_dynamic-update-slice_fusion.2
  292.4 80.0 %all-gather.13.cloned.1.call-done = bf16[1,2048,2048]{2,1,0:T(8,128)(2,1)} async-done(((bf16[1,2048,256]{2,1,0:T(8,128)(2,1)}), bf16[1,2048,2048]{2,1,0:T(8,128)(2,1)}) %all-gather.13.cloned.1.call-update) | async-done | bytes 8388624 | tf_op jit(solution)/shard_map/all_gather | solution.py:152
  372.5 5.6 fusion.76
  379.8 2.6 fusion.70
  382.4 110.4 %all-gather.15.cloned.1.call-done = bf16[1,2048,2048]{2,1,0:T(8,128)(2,1)} async-done(((bf16[1,2048,256]{2,1,0:T(8,128)(2,1)}), bf16[1,2048,2048]{2,1,0:T(8,128)(2,1)}) %all-gather.15.cloned.1.call-update) | async-done | bytes 8388624 | tf_op jit(solution)/shard_map/all_gather | solution.py:153
  492.8 5.4 fusion.64
  498.3 6.5 copy.72
  504.7 4.5 all-to-all-start
  509.3 1.8 multiply_cosine_fusion
  511.1 56.6 %all-to-all-done = bf16[7,128,2048]{1,0,2:T(8,128)(2,1)} async-done(((bf16[7,128,2048]{1,0,2:T(8,128)(2,1)}), bf16[7,128,2048]{1,0,2:T(8,128)(2,1)}, u32[]{:S(2)}, u32[]{:S(2)}) %all-to-all-start) | async-done | bytes 3670048 | tf_op jit(solution)/shard_map/all_to_all | solution.py:171
  567.7 4.8 copy.105
  572.5 1.9 fusion.121
  574.4 2.1 reshape_squeeze.15
  576.5 2.1 squeeze.56
  578.5 2.1 squeeze.55
  580.6 2.1 reshape_squeeze.14
  582.7 5.7 fusion.127
  588.4 7.2 fusion.124
  595.6 5.9 fusion.86
  601.5 14.8 %fusion.82 = f32[1024,2,128]{0,2,1:T(8,128)} fusion(bf16[1024,2,128]{0,2,1:T(8,128)(2,1)} %squeeze.55, f32[2,1024,1024]{1,2,0:T(8,128)} %fusion.127, f32[2,1024,1024]{1,2,0:T(8,128)} %get-tuple-element.78, f32[2,1024]{1,0:T(2,128)S(1)} %get-tuple-element.77), kind=kOutput, calls=%fused_computation.52 | convolution fusion | flops 551554048 | bytes 18358272 | tf_op jit(solution)/shard_map/while/body/eval_jaxpr/hqk,qhd->khd/dot_general | solution.py:118
  616.2 14.8 %fusion.79 = f32[1024,2,128]{0,2,1:T(8,128)} fusion(bf16[1024,2,128]{0,2,1:T(8,128)(2,1)} %reshape_squeeze.14, f32[2,1024,1024]{1,2,0:T(8,128)} %fusion.127, f32[2,1024,1024]{1,2,0:T(8,128)} %get-tuple-element.78, f32[2,1024]{1,0:T(2,128)S(1)} %get-tuple-element.77), kind=kOutput, calls=%fused_computation.51 | convolution fusion | flops 551554048 | bytes 18358272 | tf_op jit(solution)/shard_map/while/body/eval_jaxpr/hqk,khd->qhd/dot_general | solution.py:115
  631.1 2.1 reshape_squeeze.13
  633.1 2.1 squeeze.53
  635.2 2.1 reshape_squeeze.12
  637.3 7.2 fusion.123
  644.5 5.1 fusion.85
  649.6 3.6 copy.77
  653.7 5.6 reduce
  659.3 2.0 reshape.321
  661.3 4.4 all-to-all-start.1
  665.7 2.7 add_convert_fusion.1
  669.2 3.6 copy.88
  672.8 3.6 copy.86
  676.4 1.9 pad_maximum_fusion.6
  678.2 3.6 copy.87
  681.8 6.0 pad_maximum_fusion
  687.7 6.6 all-to-all-start.2
  694.4 3.5 reshape.322
  697.8 2.1 copy.103
  699.9 2.0 copy.78
  702.0 7.3 fusion.58
  709.2 4.0 collective-permute-start
  713.3 9.9 %all-to-all-done.2 = bf16[3,1024,256]{2,0,1:T(4,128)(2,1)} async-done(((bf16[3,1024,256]{2,0,1:T(4,128)(2,1)}), bf16[3,1024,256]{2,0,1:T(4,128)(2,1)}, u32[]{:S(2)}, u32[]{:S(2)}) %all-to-all-start.2) | async-done | bytes 1572896 | tf_op jit(solution)/shard_map/all_to_all | solution.py:135
  723.2 1.8 copy.89
  725.9 2.1 copy.92
  730.0 6.6 fusion.13
  736.6 6.5 fusion.37
  743.1 3.0 fusion.91
  746.4 2.4 collective-permute-start.1
  748.9 2.1 bitcast_convert_fusion.3
  751.0 5.9 collective-permute-done.1
  (57 shorter events, 15.9 us)
Async XLA Ops:
  7.2 124.3 %all-gather.11.cloned.1.call-start = ((), (), s32[]{:S(2)}) async-start(), calls=%async_computation.4 | async-start | bytes 9437184 | tf_op jit(solution)/shard_map/all_gather | solution.py:151
  7.9 244.0 %all-gather.9.cloned.1.call-start = ((), (), s32[]{:S(2)}) async-start(), calls=%async_computation.3 | async-start | bytes 9437184 | tf_op jit(solution)/shard_map/all_gather | solution.py:150
  8.6 363.8 %all-gather.13.cloned.1.call-start = ((), (), s32[]{:S(2)}) async-start(), calls=%async_computation.5 | async-start | bytes 9437184 | tf_op jit(solution)/shard_map/all_gather | solution.py:152
  9.4 483.4 %all-gather.15.cloned.1.call-start = ((), (), s32[]{:S(2)}) async-start(), calls=%async_computation.6 | async-start | bytes 9437184 | tf_op jit(solution)/shard_map/all_gather | solution.py:153
  251.9 12.4 %copy-start.2 = (f32[1,128,2048]{2,1,0:T(8,128)S(1)}, f32[1,128,2048]{2,1,0:T(8,128)}, u32[]{:S(2)}) copy-start(f32[1,128,2048]{2,1,0:T(8,128)} %param.9) | copy-start | bytes 3145732
  251.9 12.4 %copy-start.7 = (f32[1,2048]{1,0:T(1,128)S(1)}, f32[1,2048]{1,0:T(1,128)}, u32[]{:S(2)}) copy-start(f32[1,2048]{1,0:T(1,128)} %param.11) | copy-start | bytes 24580
  264.3 6.5 copy-start.1
  264.3 6.6 copy-start.3
  264.3 9.1 %slice-start.2 = ((s8[8388608]{0:T(1024)(128)(4,1)}), s8[4194304]{0:T(1024)(128)(4,1)S(1)}, s32[]{:S(2)}) async-start(s8[8388608]{0:T(1024)(128)(4,1)} %bitcast.208), calls=%async_computation.9 | async-start | bytes 8388608
  270.9 2.7 slice-start.3
  372.5 7.3 copy-start
  379.8 113.0 %copy-start.4 = (f32[1,128,2048]{2,1,0:T(8,128)S(1)}, f32[1,128,2048]{2,1,0:T(8,128)}, u32[]{:S(2)}) copy-start(f32[1,128,2048]{2,1,0:T(8,128)} %param.10) | copy-start | bytes 3145732
  504.7 62.9 %all-to-all-start = ((bf16[7,128,2048]{1,0,2:T(8,128)(2,1)}), bf16[7,128,2048]{1,0,2:T(8,128)(2,1)}, u32[]{:S(2)}, u32[]{:S(2)}) async-start(bf16[7,128,2048]{1,0,2:T(8,128)(2,1)} %copy.72), calls=%async_computation | async-start | bytes 8388608 | tf_op jit(solution)/shard_map/all_to_all | solution.py:171
  661.3 26.4 %all-to-all-start.1 = ((bf16[8,2,16384]{2,1,0:T(2,128)(2,1)}), bf16[8,2,16384]{2,1,0:T(2,128)(2,1)}, u32[]{:S(2)}, u32[]{:S(2)}) async-start(bf16[8,2,16384]{2,1,0:T(2,128)(2,1)} %reshape.321), calls=%async_computation.1 | async-start | bytes 1048576 | tf_op jit(solution)/shard_map/all_to_all | solution.py:135
  687.7 35.4 %all-to-all-start.2 = ((bf16[3,1024,256]{2,0,1:T(4,128)(2,1)}), bf16[3,1024,256]{2,0,1:T(4,128)(2,1)}, u32[]{:S(2)}, u32[]{:S(2)}) async-start(bf16[3,1024,256]{2,0,1:T(4,128)(2,1)} %pad_maximum_fusion), calls=%async_computation.2 | async-start | bytes 4194304 | tf_op jit(solution)/shard_map/all_to_all | solution.py:135
  709.2 39.6 %collective-permute-start = (bf16[128,2048]{1,0:T(8,128)(2,1)}, bf16[128,2048]{1,0:T(8,128)(2,1)}, u32[]{:S(2)}, u32[]{:S(2)}) collective-permute-start(bf16[128,2048]{1,0:T(8,128)(2,1)} %fusion.58), channel_id=1, source_target_pairs={{0,8},{8,16},{16,24},{24,32},{32,40},{40,48},{48,56},{56,64},{64,7... | collective-permute-start | bytes 1572872 | tf_op jit(solution)/shard_map/ppermute | solution.py:12
  729.9 6.6 copy-start.6
  729.9 13.1 %slice-start = ((s8[8388608]{0:T(1024)(128)(4,1)}), s8[4194304]{0:T(1024)(128)(4,1)S(1)}, s32[]{:S(2)}) async-start(s8[8388608]{0:T(1024)(128)(4,1)} %bitcast.204), calls=%async_computation.7 | async-start | bytes 8388608
  730.0 13.1 %copy-start.5 = (bf16[1,128,8,256]{1,3,2,0:T(8,128)(2,1)S(1)}, bf16[1,128,8,256]{1,3,2,0:T(8,128)(2,1)}, u32[]{:S(2)}) copy-start(bf16[1,128,8,256]{1,3,2,0:T(8,128)(2,1)} %copy.92) | copy-start | bytes 1572868
  736.6 6.5 slice-start.1
  746.4 10.5 %collective-permute-start.1 = (bf16[128,2048]{1,0:T(8,128)(2,1)S(1)}, bf16[128,2048]{1,0:T(8,128)(2,1)S(1)}, u32[]{:S(2)}, u32[]{:S(2)}) collective-permute-start(bf16[128,2048]{1,0:T(8,128)(2,1)S(1)} %fusion.89), channel_id=1, source_target_pairs={{0,120},{8,0},{16,8},{24,16},{32,24},{40,32},{48,40},{56,48},{64,5... | collective-permute-start | bytes 1572872 | tf_op jit(solution)/shard_map/ppermute | solution.py:12
Sparse Core Ops, SparseCore 0:
  10.2 121.2 all-gather.10
  133.6 118.2 all-gather.8
  254.1 118.3 all-gather.12
  374.5 118.2 all-gather.14
where the time goes:
time: 777 us; the launch traced here: 765 us
  waiting for transfers between devices  492 us (63%)
  matrix products  112 us (14%)
  local copies, waits for them, and re-layouts  95 us (12%)
  other arithmetic  29.8 us (4%)
  starting transfers between devices  22.1 us (3%)
  between operations  14.4 us (2%)
    all_gather x1, waiting for transfers between devices, shards(): lax.all_gather(w_key[0], 'seq', axis=1, tiled=True)  118 us
    all_gather x1, waiting for transfers between devices, shards(): lax.all_gather(w_out[0], 'seq', axis=1, tiled=True)  110 us
    all_gather x1, waiting for transfers between devices, shards(): lax.all_gather(w_query[0], 'seq', axis=1, tiled=True)  108 us
    all_gather x1, waiting for transfers between devices, shards(): lax.all_gather(w_value[0], 'seq', axis=1, tiled=True)  80 us
    all_to_all x1, waiting for transfers between devices, shards(): lax.all_to_all(pieces, 'seq', split_axis=2, concat_axis=1, tiled=True)  56.6 us
    dot_general x4, matrix products, times_t(): lax.dot_general(left, right, (((1,), (1,)), ((), ())), preferred_element_...  23.4 us
  transfers between devices with their start and end apart: 9, of which 7 were waited for; matrix products, arithmetic and copies ran while one was open for 17% of the time, Pallas kernels for 0%

commit v1 on v0

--- a/solution.py
+++ b/solution.py
@@ -149,7 +149,7 @@
     all_query, all_key, all_value, all_out = (
         lax.all_gather(w_query[0], "seq", axis=1, tiled=True),
         lax.all_gather(w_key[0], "seq", axis=1, tiled=True),
-        lax.all_gather(w_value[0], "seq", axis=1, tiled=True),
+        jnp.concatenate(lax.all_gather(w_value[0], "seq"), axis=1),
         lax.all_gather(w_out[0], "seq", axis=1, tiled=True),
     )
     local_cos, local_sin = rope_tables(lax.axis_index("seq") * local_rows + jnp.arange(local_rows))

time: 777 us -> 730 us (0.940)
  waiting for transfers between devices: 492 us -> 470 us
  local copies, waits for them, and re-layouts: 95 us -> 79 us
    all_gather x1, waiting for transfers between devices: 110 us -> 91.9 us  [shards(): lax.all_gather(w_out[0], 'seq', axis=1, tiled=True)]
    all_gather x0 -> x1, local copies, waits for them, and re-layouts: none -> 11.8 us  [shards(): lax.all_gather(w_value[0], 'seq')]
  transfers between devices with their start and end apart: 9 -> 9, of which waited for: 7 -> 7; matrix products, arithmetic and copies ran while one was open for 17% -> 18% of each run, Pallas kernels for 0% -> 0%
where the time goes in v1:
time: 730 us; the launch traced here: 719 us
  waiting for transfers between devices  470 us (64%)
  matrix products  106 us (15%)
  local copies, waits for them, and re-layouts  79 us (11%)
  other arithmetic  28.4 us (4%)
  starting transfers between devices  22.1 us (3%)
  between operations  14.6 us (2%)
    all_gather x1, waiting for transfers between devices, shards(): lax.all_gather(w_key[0], 'seq', axis=1, tiled=True)  117 us
    all_gather x1, waiting for transfers between devices, shards(): lax.all_gather(w_query[0], 'seq', axis=1, tiled=True)  109 us
    all_gather x1, waiting for transfers between devices, shards(): lax.all_gather(w_out[0], 'seq', axis=1, tiled=True)  91.9 us
    all_gather x1, waiting for transfers between devices, shards(): lax.all_gather(w_value[0], 'seq')  77.5 us
    all_to_all x1, waiting for transfers between devices, shards(): lax.all_to_all(pieces, 'seq', split_axis=2, concat_axis=1, tiled=True)  56.6 us
    dot_general x4, matrix products, times_t(): lax.dot_general(left, right, (((1,), (1,)), ((), ())), preferred_element_...  21.6 us
    dot_general x1, matrix products, step(): jnp.einsum('hqk,qhd->khd', score_grad, query_block, preferred_element_typ...  14.7 us
  transfers between devices with their start and end apart: 9, of which 7 were waited for; matrix products, arithmetic and copies ran while one was open for 18% of the time, Pallas kernels for 0%

profile of v1, /device:TPU:1, one launch (start us, length us, event | category | flops | bytes accessed | tf_op | source)
XLA Modules:
  0.0 719.4 jit_solution(18219292756745799930)
XLA Ops:
  10.0 1.4 fusion.65
  11.4 1.4 fusion.71
  13.0 1.8 multiply_convert_fusion.1
  14.8 116.7 %all-gather.12.cloned.1.call-done = bf16[1,2048,2048]{2,1,0:T(8,128)(2,1)} async-done(((bf16[1,2048,256]{2,1,0:T(8,128)(2,1)}), bf16[1,2048,2048]{2,1,0:T(8,128)(2,1)}) %all-gather.12.cloned.1.call-update) | async-done | bytes 8388624 | tf_op jit(solution)/shard_map/all_gather | solution.py:151
  131.5 11.9 %copy.69 = bf16[2048,2048]{1,0:T(8,128)(2,1)} copy(bf16[2048,2048]{0,1:T(8,128)(2,1)} %bitcast.201) | data formatting | bytes 16777216 | tf_op jit(solution)/shard_map/dot_general | solution.py:162
  143.3 108.6 %all-gather.10.cloned.1.call-done = bf16[1,2048,2048]{2,1,0:T(8,128)(2,1)} async-done(((bf16[1,2048,256]{2,1,0:T(8,128)(2,1)}), bf16[1,2048,2048]{2,1,0:T(8,128)(2,1)}) %all-gather.10.cloned.1.call-update) | async-done | bytes 8388624 | tf_op jit(solution)/shard_map/all_gather | solution.py:150
  251.9 12.3 %copy.68 = bf16[2048,2048]{1,0:T(8,128)(2,1)} copy(bf16[2048,2048]{0,1:T(8,128)(2,1)} %bitcast.202) | data formatting | bytes 16777216 | tf_op jit(solution)/shard_map/dot_general | solution.py:159
  264.2 6.6 fusion.76
  270.8 2.4 fusion.81
  273.4 2.4 fusion.78
  275.8 2.4 fusion.83
  278.2 1.5 subtract_convert_fusion.2
  280.2 1.1 pad_maximum_fusion.3
  281.5 1.8 pad_maximum_fusion.4
  283.3 1.2 copy.74
  284.6 77.5 %all-gather.8.cloned.1.call-done = bf16[8,2048,256]{2,1,0:T(8,128)(2,1)} async-done(((bf16[1,2048,256]{2,1,0:T(8,128)(2,1)}), bf16[8,2048,256]{2,1,0:T(8,128)(2,1)}) %all-gather.8.cloned.1.call-update) | async-done | bytes 8388624 | tf_op jit(solution)/shard_map/all_gather | solution.py:152
  362.1 11.8 %copy.70 = bf16[8,2048,256]{1,2,0:T(8,128)(2,1)} copy(bf16[8,2048,256]{2,1,0:T(8,128)(2,1)} %all-gather.8.cloned.1.call-done) | data formatting | bytes 16777216 | tf_op jit(solution)/shard_map/all_gather | solution.py:152
  374.8 0.9 constant_dynamic-update-slice_fusion.2
  375.6 7.9 %fusion.45 = bf16[7,128,2048]{2,1,0:T(8,128)(2,1)} fusion(bf16[7,128,2048]{2,1,0:T(8,128)(2,1)} %constant_dynamic-update-slice_fusion.2, bf16[2048,2048]{0,1:T(8,128)(2,1)} %bitcast.190, bf16[1,128,2048]{2,1,0:T(8,128)(2,1)S(1)} %get-tuple-element.72), kind=kOutput, calls=%fused_computation.39 | convolution fusion | flops 1074003968 | bytes 9437184 | tf_op jit(solution)/shard_map/dot_general | solution.py:164
  384.4 0.9 constant_dynamic-update-slice_fusion
  385.3 3.7 fusion.47
  389.0 91.9 %all-gather.14.cloned.1.call-done = bf16[1,2048,2048]{2,1,0:T(8,128)(2,1)} async-done(((bf16[1,2048,256]{2,1,0:T(8,128)(2,1)}), bf16[1,2048,2048]{2,1,0:T(8,128)(2,1)}) %all-gather.14.cloned.1.call-update) | async-done | bytes 8388624 | tf_op jit(solution)/shard_map/all_gather | solution.py:153
  480.9 5.4 fusion.51
  486.3 6.5 copy.75
  492.8 4.5 all-to-all-start
  497.3 1.8 multiply_cosine_fusion
  499.1 56.6 %all-to-all-done = bf16[7,128,2048]{1,0,2:T(8,128)(2,1)} async-done(((bf16[7,128,2048]{1,0,2:T(8,128)(2,1)}), bf16[7,128,2048]{1,0,2:T(8,128)(2,1)}, u32[]{:S(2)}, u32[]{:S(2)}) %all-to-all-start) | async-done | bytes 3670048 | tf_op jit(solution)/shard_map/all_to_all | solution.py:171
  555.7 4.8 copy.108
  560.5 1.0 fusion.93
  561.6 2.1 squeeze.52
  563.6 1.1 squeeze.51
  564.7 1.0 reshape_squeeze.14
  565.9 7.2 %fusion.96 = (f32[2,1024]{1,0:T(2,128)S(1)}, f32[2,1024,1024]{1,2,0:T(8,128)}) fusion(bf16[1024,2,128]{0,2,1:T(8,128)(2,1)} %squeeze.51, bf16[1024,2,128]{0,2,1:T(8,128)(2,1)} %reshape_squeeze.14), kind=kOutput, calls=%fused_computation.120 | convolution fusion | flops 543163392 | bytes 9445376 | tf_op jit(solution)/shard_map/while/body/eval_jaxpr/sub | solution.py:103
  573.2 5.4 fusion.99
  579.2 2.3 fusion.61
  581.5 12.5 %fusion.54 = f32[1024,2,128]{0,2,1:T(8,128)S(1)} fusion(bf16[1024,2,128]{0,2,1:T(8,128)(2,1)} %reshape_squeeze.14, f32[2,1024,1024]{1,2,0:T(8,128)} %fusion.99, f32[2,1024,1024]{1,2,0:T(8,128)} %get-tuple-element.80, f32[2,1024]{1,0:T(2,128)S(1)} %get-tuple-element.79), kind=kOutput, calls=%fused_computation.45 | convolution fusion | flops 551554048 | bytes 18358272 | tf_op jit(solution)/shard_map/while/body/eval_jaxpr/hqk,khd->qhd/dot_general | solution.py:115
  594.1 14.7 %fusion.57 = f32[1024,2,128]{0,2,1:T(8,128)} fusion(bf16[1024,2,128]{0,2,1:T(8,128)(2,1)} %squeeze.51, f32[2,1024,1024]{1,2,0:T(8,128)} %fusion.99, f32[2,1024,1024]{1,2,0:T(8,128)} %get-tuple-element.80, f32[2,1024]{1,0:T(2,128)S(1)} %get-tuple-element.79), kind=kOutput, calls=%fused_computation.46 | convolution fusion | flops 551554048 | bytes 18358272 | tf_op jit(solution)/shard_map/while/body/eval_jaxpr/hqk,qhd->khd/dot_general | solution.py:118
  608.8 1.0 reshape_squeeze.12
  610.1 1.0 reshape_squeeze.13
  611.1 7.1 fusion.95
  618.1 4.2 fusion.60
  622.3 0.9 copy.80
  623.7 3.8 reduce
  627.5 0.9 reshape.356
  628.4 4.4 all-to-all-start.1
  632.8 2.4 add_convert_fusion.1
  635.2 2.4 copy.91
  638.5 1.9 pad_maximum_fusion.5
  640.5 3.6 copy.89
  644.0 5.6 pad_maximum_fusion
  649.7 6.6 all-to-all-start.2
  656.3 3.5 reshape.357
  659.7 2.1 copy.106
  661.8 2.0 copy.81
  663.9 7.3 %fusion.41 = bf16[128,2048]{1,0:T(8,128)(2,1)} fusion(bf16[128,2048]{0,1:T(8,128)(2,1)} %bitcast.211, bf16[1,2048,2048]{2,1,0:T(8,128)(2,1)} %all-gather.14.cloned.1.call-done, f32[1,128,2048]{2,1,0:T(8,128)S(1)} %copy-done.3), kind=kOutput, calls=%fused_computation.37 | convolution fusion | flops 1074266112 | bytes 10485760 | tf_op jit(solution)/shard_map/dot_general | solution.py:56
  671.2 4.0 collective-permute-start
  675.2 9.9 %all-to-all-done.2 = bf16[3,1024,256]{2,0,1:T(4,128)(2,1)S(1)} async-done(((bf16[3,1024,256]{2,0,1:T(4,128)(2,1)}), bf16[3,1024,256]{2,0,1:T(4,128)(2,1)S(1)}, u32[]{:S(2)}, u32[]{:S(2)}) %all-to-all-start.2) | async-done | bytes 1572896 | tf_op jit(solution)/shard_map/all_to_all | solution.py:135
  686.3 6.5 fusion.7
  692.7 6.5 fusion.31
  699.3 1.4 fusion.70
  701.0 2.4 collective-permute-start.1
  703.4 2.1 bitcast_convert_fusion.3
  705.5 5.9 collective-permute-done.1
  711.4 1.1 bitcast_convert_fusion.2
  (66 shorter events, 9.5 us)
Async XLA Ops:
  7.2 124.3 %all-gather.12.cloned.1.call-start = ((), (), s32[]{:S(2)}) async-start(), calls=%async_computation.5 | async-start | bytes 9437184 | tf_op jit(solution)/shard_map/all_gather | solution.py:151
  7.9 244.0 %all-gather.10.cloned.1.call-start = ((), (), s32[]{:S(2)}) async-start(), calls=%async_computation.4 | async-start | bytes 9437184 | tf_op jit(solution)/shard_map/all_gather | solution.py:150
  8.6 353.5 %all-gather.8.cloned.1.call-start = ((), (), s32[]{:S(2)}) async-start(), calls=%async_computation.3 | async-start | bytes 9437184 | tf_op jit(solution)/shard_map/all_gather | solution.py:152
  9.4 471.5 %all-gather.14.cloned.1.call-start = ((), (), s32[]{:S(2)}) async-start(), calls=%async_computation.6 | async-start | bytes 9437184 | tf_op jit(solution)/shard_map/all_gather | solution.py:153
  264.2 6.6 copy-start.1
  264.2 9.0 %slice-start.2 = ((s8[8388608]{0:T(1024)(128)(4,1)}), s8[4194304]{0:T(1024)(128)(4,1)S(1)}, s32[]{:S(2)}) async-start(s8[8388608]{0:T(1024)(128)(4,1)} %bitcast.197), calls=%async_computation.9 | async-start | bytes 8388608
  270.8 2.6 slice-start.3
  373.9 11.4 %copy-start = (bf16[8,2048,256]{1,2,0:T(8,128)(2,1)S(1)}, bf16[8,2048,256]{1,2,0:T(8,128)(2,1)}, u32[]{:S(2)}) copy-start(bf16[8,2048,256]{1,2,0:T(8,128)(2,1)} %copy.70) | copy-start | bytes 25165828
  375.6 105.2 %copy-start.4 = (f32[1,128,2048]{2,1,0:T(8,128)S(1)}, f32[1,128,2048]{2,1,0:T(8,128)}, u32[]{:S(2)}) copy-start(f32[1,128,2048]{2,1,0:T(8,128)} %param.10) | copy-start | bytes 3145732
  492.8 62.9 %all-to-all-start = ((bf16[7,128,2048]{1,0,2:T(8,128)(2,1)}), bf16[7,128,2048]{1,0,2:T(8,128)(2,1)}, u32[]{:S(2)}, u32[]{:S(2)}) async-start(bf16[7,128,2048]{1,0,2:T(8,128)(2,1)} %copy.75), calls=%async_computation | async-start | bytes 8388608 | tf_op jit(solution)/shard_map/all_to_all | solution.py:171
  564.7 8.5 %copy-start.6 = (bf16[1024,2,128]{0,2,1:T(8,128)(2,1)S(1)}, bf16[1024,2,128]{0,2,1:T(8,128)(2,1)}, u32[]{:S(2)}) copy-start(bf16[1024,2,128]{0,2,1:T(8,128)(2,1)} %squeeze.52) | copy-start | bytes 1572868
  573.2 6.1 copy-start.10
  610.0 8.1 %copy-start.8 = (bf16[1024,2,128]{0,2,1:T(8,128)(2,1)S(1)}, bf16[1024,2,128]{0,2,1:T(8,128)(2,1)}, u32[]{:S(2)}) copy-start(bf16[1024,2,128]{0,2,1:T(8,128)(2,1)} %reshape_squeeze.12) | copy-start | bytes 1572868
  618.1 14.7 %copy-start.7 = (f32[1024,64]{0,1:T(8,128)S(1)}, f32[1024,64]{0,1:T(8,128)}, u32[]{:S(2)}) copy-start(f32[1024,64]{0,1:T(8,128)} %get-tuple-element.74) | copy-start | bytes 786436
  628.4 21.2 %all-to-all-start.1 = ((bf16[8,2,16384]{2,1,0:T(2,128)(2,1)}), bf16[8,2,16384]{2,1,0:T(2,128)(2,1)}, u32[]{:S(2)}, u32[]{:S(2)}) async-start(bf16[8,2,16384]{2,1,0:T(2,128)(2,1)} %reshape.356), calls=%async_computation.1 | async-start | bytes 1048576 | tf_op jit(solution)/shard_map/all_to_all | solution.py:135
  638.5 25.4 %copy-start.3 = (f32[1,128,2048]{2,1,0:T(8,128)S(1)}, f32[1,128,2048]{2,1,0:T(8,128)}, u32[]{:S(2)}) copy-start(f32[1,128,2048]{2,1,0:T(8,128)} %param.8) | copy-start | bytes 3145732
  649.7 35.4 %all-to-all-start.2 = ((bf16[3,1024,256]{2,0,1:T(4,128)(2,1)}), bf16[3,1024,256]{2,0,1:T(4,128)(2,1)S(1)}, u32[]{:S(2)}, u32[]{:S(2)}) async-start(bf16[3,1024,256]{2,0,1:T(4,128)(2,1)} %pad_maximum_fusion), calls=%async_computation.2 | async-start | bytes 4194304 | tf_op jit(solution)/shard_map/all_to_all | solution.py:135
  671.2 32.2 %collective-permute-start = (bf16[128,2048]{1,0:T(8,128)(2,1)}, bf16[128,2048]{1,0:T(8,128)(2,1)}, u32[]{:S(2)}, u32[]{:S(2)}) collective-permute-start(bf16[128,2048]{1,0:T(8,128)(2,1)} %fusion.41), channel_id=1, source_target_pairs={{0,8},{8,16},{16,24},{24,32},{32,40},{40,48},{48,56},{56,64},{64,7... | collective-permute-start | bytes 1572872 | tf_op jit(solution)/shard_map/ppermute | solution.py:12
  686.2 13.0 %slice-start = ((s8[8388608]{0:T(1024)(128)(4,1)}), s8[4194304]{0:T(1024)(128)(4,1)S(1)}, s32[]{:S(2)}) async-start(s8[8388608]{0:T(1024)(128)(4,1)} %bitcast.192), calls=%async_computation.7 | async-start | bytes 8388608
  686.2 13.0 %copy-start.2 = (f32[1,128,2048]{2,1,0:T(8,128)S(1)}, f32[1,128,2048]{2,1,0:T(8,128)}, u32[]{:S(2)}) copy-start(f32[1,128,2048]{2,1,0:T(8,128)} %param.9) | copy-start | bytes 3145732
  686.3 13.0 %copy-start.9 = (f32[1,2048]{1,0:T(1,128)S(1)}, f32[1,2048]{1,0:T(1,128)}, u32[]{:S(2)}) copy-start(f32[1,2048]{1,0:T(1,128)} %param.11) | copy-start | bytes 24580
  692.7 6.5 slice-start.1
  699.3 1.4 copy-start.5
  701.0 10.4 %collective-permute-start.1 = (bf16[128,2048]{1,0:T(8,128)(2,1)S(1)}, bf16[128,2048]{1,0:T(8,128)(2,1)S(1)}, u32[]{:S(2)}, u32[]{:S(2)}) collective-permute-start(bf16[128,2048]{1,0:T(8,128)(2,1)S(1)} %fusion.64), channel_id=1, source_target_pairs={{0,120},{8,0},{16,8},{24,16},{32,24},{40,32},{48,40},{56,48},{64,5... | collective-permute-start | bytes 1572872 | tf_op jit(solution)/shard_map/ppermute | solution.py:12
Sparse Core Ops, SparseCore 0:
  10.2 121.2 all-gather.11
  133.6 118.2 all-gather.9
  254.3 107.7 all-gather.7
  364.1 116.6 all-gather.13
